TPU v7x, 32 devices: a whole 2x2x4 slice. The times are simulated.
32 devices in a mesh: region: 8 (over z, core), state: 4 (over y, x).
Axes of the slice: x: 2, y: 2, z: 4, core: 2. Of those that a mesh axis runs over, the one named last changes fastest.
Arguments:
- state_anom: float32 [8, 16, 256, 512], P('region', 'state'), may hold values from -6 to 6
- obs_anom: float32 [8, 256, 512], P('region', 'state'), may hold values from -6 to 6
- obs_weight: float32 [8, 256, 512], P('region', 'state'), may hold values from -6 to 6
- obs_cell: int32 [8, 256], P('region', 'state'), may hold values from 0 to 255, as said below
- sector_of: int32 [8], replicated, may hold values from 0 to 7, as said below
Outputs:
- increment: float32 [8, 16, 256, 512], P('region', 'state')
Inputs may be any that keep to these rules, and one draw needn't show every extreme that they name: `obs_cell`: each entry is lon * 8 + lat with lon in 0..31 and lat in 0..7. Within each aligned block of 64 entries along the observation dimension the entries do not decrease; in each such block between 8 and 16 entries have lon < 8, and between 8 and 16 have lon >= 24; the bound 16 is reached on both sides in every draw. `sector_of`: A permutation: every region holds a different sector.
All inputs are finite; a program needn't handle non-finite values.
Results may differ from a plain program's by a relative error of at most 0.0003.
Values sent between devices are 32-bit elements; how exact they have to be, the bound alone decides.
No kernel may reach another device: no remote copies, remote signals or barrier semaphores. Data moves between devices by JAX's collectives and lax.ppermute only.
A program may use at most 64 MiB of HBM per device.

v0:
```python
import jax
import jax.numpy as jnp
from jax import lax
from jax.sharding import PartitionSpec as P

SECT_W = 32
LAT = 8
HALF = 4
CAP = 16
COLS = 256


def gaspari(scaled):
    inside = scaled * scaled * (scaled * (scaled * (0.5 - 0.25 * scaled) + 0.625) - 5.0 / 3.0) + 1.0
    floored = jnp.maximum(scaled, 1.0)
    outside = (
        scaled * (scaled * (scaled * (scaled * (scaled / 12.0 - 0.5) + 0.625) + 5.0 / 3.0) - 5.0)
        + 4.0
        - 2.0 / (3.0 * floored)
    )
    return jnp.where(scaled <= 1.0, inside, jnp.where(scaled < 2.0, outside, 0.0))


def taper_tile(state_cells, obs_cells, lon_span):
    state_lon = state_cells // LAT
    state_lat = state_cells % LAT
    obs_lon = obs_cells // LAT
    obs_lat = obs_cells % LAT
    lon_gap = state_lon[:, None] - obs_lon[None, :]
    lon_gap = (lon_gap + lon_span + lon_span // 2) % lon_span - lon_span // 2
    lat_gap = state_lat[:, None] - obs_lat[None, :]
    scaled = jnp.sqrt((lon_gap * lon_gap + lat_gap * lat_gap).astype(jnp.float32)) / HALF
    return gaspari(scaled)


def add_block(flat_state, state_cells, pieces, lon_span):
    piece_anom, piece_weight, piece_cells = pieces
    covar = jnp.einsum("rm,pm->rp", flat_state, piece_anom, precision=lax.Precision.HIGHEST)
    columns = state_cells.shape[0]
    levels_here = flat_state.shape[0] // columns
    tile = taper_tile(state_cells, piece_cells, lon_span) / (flat_state.shape[1] - 1)
    covar = (covar.reshape(levels_here, columns, -1) * tile[None]).reshape(flat_state.shape[0], -1)
    return jnp.dot(covar, piece_weight, precision=lax.Precision.HIGHEST)


def on_device(state_anom, obs_anom, obs_weight, obs_cell, sector_of):
    regions = lax.axis_size("region")
    lon_span = regions * SECT_W
    region_ids = jnp.arange(regions, dtype=jnp.int32)
    my_region = lax.axis_index("region")
    my_sector = jnp.sum(jnp.where(region_ids == my_region, sector_of, 0))
    left_region = jnp.sum(
        jnp.where(sector_of == (my_sector + regions - 1) % regions, region_ids, 0)
    )
    right_region = jnp.sum(jnp.where(sector_of == (my_sector + 1) % regions, region_ids, 0))
    own_anom = obs_anom[0]
    own_weight = obs_weight[0]
    own_cells = obs_cell[0] + my_sector * (SECT_W * LAT)
    count = own_anom.shape[0]
    low_set = (own_anom[:CAP], own_weight[:CAP], own_cells[:CAP])
    high_set = (own_anom[count - CAP :], own_weight[count - CAP :], own_cells[count - CAP :])
    to_left = region_ids == left_region
    to_right = region_ids == right_region

    def place(first, second):
        shaped = (regions,) + (1,) * first.ndim
        return jnp.where(to_left.reshape(shaped), first[None], 0) + jnp.where(
            to_right.reshape(shaped), second[None], 0
        )

    slotted = (
        lax.all_to_all(
            place(low_set[0], high_set[0]), "region", split_axis=0, concat_axis=0, tiled=True
        ),
        lax.all_to_all(
            place(low_set[1], high_set[1]), "region", split_axis=0, concat_axis=0, tiled=True
        ),
        lax.all_to_all(
            place(low_set[2], high_set[2]), "region", split_axis=0, concat_axis=0, tiled=True
        ),
    )
    from_left = tuple(
        (lax.dynamic_index_in_dim(pieces, left_region, 0, keepdims=False) for pieces in slotted)
    )
    from_right = tuple(
        (lax.dynamic_index_in_dim(pieces, right_region, 0, keepdims=False) for pieces in slotted)
    )
    halo_set = tuple(
        (
            jnp.concatenate([left_part, right_part], axis=0)
            for left_part, right_part in zip(from_left, from_right)
        )
    )
    flat_state = state_anom[0].reshape(-1, state_anom.shape[-1])
    state_cells = my_sector * (SECT_W * LAT) + jnp.arange(COLS, dtype=jnp.int32)
    joined = tuple(
        (
            jnp.concatenate([own_part, halo_part], axis=0)
            for own_part, halo_part in zip((own_anom, own_weight, own_cells), halo_set)
        )
    )
    total = add_block(
        flat_state,
        state_cells,
        (
            lax.all_gather(joined[0], "state", axis=0, tiled=True),
            lax.all_gather(joined[1], "state", axis=0, tiled=True),
            lax.all_gather(joined[2], "state", axis=0, tiled=True),
        ),
        lon_span,
    )
    return total.reshape(state_anom.shape)


def solution(mesh):
    in_specs = (
        P("region", "state", None, None),
        P("region", "state", None),
        P("region", "state", None),
        P("region", "state"),
        P(),
    )
    out_specs = P("region", "state", None, None)
    return jax.shard_map(
        on_device, mesh=mesh, in_specs=in_specs, out_specs=out_specs, check_vma=False
    )
```

profile of v0, /device:TPU:0, one launch (start us, length us, event | category | flops | bytes accessed | tf_op | source)
XLA Modules:
  0.0 79.8 jit_solution(260493578877022644)
XLA Ops:
  0.0 0.0 copy-start
  0.0 1.4 %fusion.13 = s32[]{:T(128)} fusion(s32[8]{0:T(128)} %param.9, s32[]{:T(128)S(6)} %axis_index.15), kind=kLoop, calls=%fused_computation.55 | loop fusion | flops 23 | bytes 40 | tf_op jit(solution)/shard_map/reduce_sum | solution.py:51
  3.4 0.7 broadcast_add_fusion
  4.1 0.1 slice_bitcast_fusion.5
  4.2 1.4 %fusion.15 = (s32[]{:T(128)}, s32[]{:T(128)}) fusion(s32[8]{0:T(128)} %param.9, s32[]{:T(128)S(6)} %select_n.127, s32[]{:T(128)S(6)} %select_n.124), kind=kLoop, calls=%fused_computation.57 | loop fusion | flops 46 | bytes 48 | tf_op jit(solution)/shard_map/reduce_sum | solution.py:55
  5.5 1.2 %iota_compare_fusion = (pred[8]{0:T(512)(128)(4,1)S(1)}, pred[8]{0:T(512)(128)(4,1)S(1)}) fusion(s32[]{:T(128)} %get-tuple-element.5, s32[]{:T(128)} %get-tuple-element.6), kind=kLoop, calls=%fused_computation.62 | loop fusion | flops 16 | bytes 24 | tf_op jit(solution)/shard_map/eq | solution.py:63
  6.8 0.7 fusion.8
  7.4 6.4 %all-to-all-start.1 = ((s32[8,1,16]{2,1,0:T(1,128)}), s32[8,1,16]{2,1,0:T(1,128)S(1)}, u32[]{:S(2)}, u32[]{:S(2)}) async-start(s32[8,1,16]{2,1,0:T(1,128)} %fusion.8), calls=%async_computation.1 | async-start | bytes 8192 | tf_op jit(solution)/shard_map/all_to_all | solution.py:78
  13.8 0.7 fusion.19
  14.5 0.8 %slice_bitcast_fusion.1 = (f32[16,512]{1,0:T(8,128)S(1)}, f32[16,512]{1,0:T(8,128)S(1)}, f32[16,512]{1,0:T(8,128)S(1)}, f32[16,512]{1,0:T(8,128)S(1)}) fusion(f32[1,64,512]{2,1,0:T(8,128)} %param.7, f32[1,64,512]{2,1,0:T(8,128)} %param.6), kind=kLoop, calls=%fused_computation.25 | loop fusion | bytes 262144 | tf_op jit(solution)/shard_map/jit(_where)/broadcast_in_dim | solution.py:67
  15.3 0.9 %select_add_fusion = (f32[8,16,512]{2,1,0:T(8,128)}, f32[8,16,512]{2,1,0:T(8,128)}) fusion(f32[16,512]{1,0:T(8,128)S(1)} %get-tuple-element.12, f32[16,512]{1,0:T(8,128)S(1)} %get-tuple-element.11, pred[8]{0:T(512)(128)(4,1)S(1)} %get-tuple-element.25, pred[8]{0:T(512)(128)(4,1)S(1)} %get-tuple-element.26, f32[16,512]{1,0:T(8,128)S(1)} %get-tuple-element.27, ...), kind=kLoop, calls=%fused_computation.18 | loop fusion | flops 393216 | bytes 655376 | tf_op jit(solution)/shard_map/add | solution.py:67
  20.0 1.3 %dynamic-slice.2 = u32[1]{0:T(128)} dynamic-slice(u32[32]{0:T(128)} %constant.145, u32[]{:T(128)S(6)} %add.195), dynamic_slice_sizes={1} | dynamic-slice | bytes 12
  21.9 0.0 all-to-all-done.1
  21.9 5.1 %all-to-all-start = ((f32[8,16,512]{2,1,0:T(8,128)}), f32[8,16,512]{2,1,0:T(8,128)S(1)}, u32[]{:S(2)}, u32[]{:S(2)}) async-start(f32[8,16,512]{2,1,0:T(8,128)} %get-tuple-element.20), calls=%async_computation | async-start | bytes 524288 | tf_op jit(solution)/shard_map/all_to_all | solution.py:72
  27.1 0.2 add_dynamic-update-slice_fusion
  27.2 7.4 %all-reduce = s32[384]{0:T(512)S(1)} all-reduce(s32[384]{0:T(512)S(1)} %add_dynamic-update-slice_fusion), channel_id=1, replica_groups=mesh['region'=8,'state'=4] {'state'}, use_global_device_ids=true, to_apply=%add | all-reduce | flops 384 | bytes 3072
  34.6 0.8 %select_multiply_fusion = f32[256,384]{0,1:T(8,128)S(1)} fusion(s32[384]{0:T(512)S(1)} %get-tuple-element.18, s32[256]{0:T(256)S(1)} %get-tuple-element.23, s32[384]{0:T(512)S(1)} %get-tuple-element.17, s32[256]{0:T(256)S(1)} %get-tuple-element.24), kind=kLoop, calls=%fused_computation.12 | loop fusion | flops 4718592 | bytes 398336 | tf_op jit(solution)/shard_map/div | solution.py:41
  35.4 0.3 mul.120
  35.7 0.0 copy-start.1
  35.7 1.5 %copy.8 = f32[48,8,4,256]{3,1,2,0:T(8,128)} copy(f32[48,8,4,256]{3,2,1,0:T(4,128)S(1)} %bitcast.48) | data formatting | bytes 3145728
  37.2 0.0 all-to-all-done
  37.2 5.1 %all-to-all-start.2 = ((f32[8,16,512]{2,1,0:T(8,128)}), f32[8,16,512]{2,1,0:T(8,128)S(1)}, u32[]{:S(2)}, u32[]{:S(2)}) async-start(f32[8,16,512]{2,1,0:T(8,128)} %get-tuple-element.19), calls=%async_computation.2 | async-start | bytes 524288 | tf_op jit(solution)/shard_map/all_to_all | solution.py:75
  42.3 0.0 copy-done.1
  42.3 12.7 %all_gather.9 = f32[384,512]{1,0:T(8,128)S(1)} all-gather(f32[96,512]{1,0:T(8,128)S(1)} %pad_maximum_fusion), channel_id=1, replica_groups=mesh['region'=8,'state'=4] {'state'}, dimensions={0}, use_global_device_ids=true | all-gather | bytes 983040 | tf_op jit(solution)/shard_map/all_gather | solution.py:106
  55.0 0.0 copy-done
  55.0 5.3 %bitcast_multiply_fusion = f32[1024,384]{0,1:T(8,128)} fusion(f32[1024,384]{0,1:T(8,128)} %bitcast.47, f32[384,512]{1,0:T(8,128)S(1)} %all_gather.9, f32[1024,512]{1,0:T(8,128)S(1)} %bitcast.45), kind=kOutput, calls=%fused_computation.1 | convolution fusion | flops 2416312320 | bytes 6029312 | tf_op jit(solution)/shard_map/rm,pm->rp/dot_general | solution.py:38
  60.4 0.0 copy-start.2
  60.4 3.1 %copy.7 = f32[1024,384]{1,0:T(8,128)} copy(f32[1024,384]{0,1:T(8,128)} %bitcast_multiply_fusion) | data formatting | bytes 3145728 | tf_op jit(solution)/shard_map/reshape.79
  63.4 0.0 all-to-all-done.2
  63.4 0.0 copy-done.2
  63.5 10.1 %all_gather.11 = f32[384,512]{1,0:T(8,128)S(1)} all-gather(f32[96,512]{1,0:T(8,128)S(1)} %pad_maximum_fusion.1), channel_id=1, replica_groups=mesh['region'=8,'state'=4] {'state'}, dimensions={0}, use_global_device_ids=true | all-gather | bytes 983040 | tf_op jit(solution)/shard_map/all_gather | solution.py:107
  73.6 6.2 %convolution_bitcast_fusion = f32[1,4,256,512]{3,2,1,0:T(8,128)} fusion(f32[4,256,384]{2,1,0:T(8,128)} %bitcast.46, f32[384,512]{1,0:T(8,128)S(1)} %all_gather.11), kind=kOutput, calls=%fused_computation | convolution fusion | flops 2415919104 | bytes 4456448 | tf_op jit(solution)/shard_map/dot_general | solution.py:43
  (8 shorter events, 0.1 us)
Async XLA Ops:
  0.0 55.0 %copy-start = (f32[1,4,256,512]{3,2,1,0:T(8,128)S(1)}, f32[1,4,256,512]{3,2,1,0:T(8,128)}, u32[]{:S(2)}) copy-start(f32[1,4,256,512]{3,2,1,0:T(8,128)} %param.5) | copy-start | bytes 6291460
  7.4 14.5 %all-to-all-start.1 = ((s32[8,1,16]{2,1,0:T(1,128)}), s32[8,1,16]{2,1,0:T(1,128)S(1)}, u32[]{:S(2)}, u32[]{:S(2)}) async-start(s32[8,1,16]{2,1,0:T(1,128)} %fusion.8), calls=%async_computation.1 | async-start | bytes 8192 | tf_op jit(solution)/shard_map/all_to_all | solution.py:78
  21.9 15.3 %all-to-all-start = ((f32[8,16,512]{2,1,0:T(8,128)}), f32[8,16,512]{2,1,0:T(8,128)S(1)}, u32[]{:S(2)}, u32[]{:S(2)}) async-start(f32[8,16,512]{2,1,0:T(8,128)} %get-tuple-element.20), calls=%async_computation | async-start | bytes 524288 | tf_op jit(solution)/shard_map/all_to_all | solution.py:72
  35.7 6.6 %copy-start.1 = (f32[1,64,512]{2,1,0:T(8,128)S(1)}, f32[1,64,512]{2,1,0:T(8,128)}, u32[]{:S(2)}) copy-start(f32[1,64,512]{2,1,0:T(8,128)} %param.6) | copy-start | bytes 393220
  37.2 26.2 %all-to-all-start.2 = ((f32[8,16,512]{2,1,0:T(8,128)}), f32[8,16,512]{2,1,0:T(8,128)S(1)}, u32[]{:S(2)}, u32[]{:S(2)}) async-start(f32[8,16,512]{2,1,0:T(8,128)} %get-tuple-element.19), calls=%async_computation.2 | async-start | bytes 524288 | tf_op jit(solution)/shard_map/all_to_all | solution.py:75
  60.4 3.1 %copy-start.2 = (f32[1,64,512]{2,1,0:T(8,128)S(1)}, f32[1,64,512]{2,1,0:T(8,128)}, u32[]{:S(2)}) copy-start(f32[1,64,512]{2,1,0:T(8,128)} %param.7) | copy-start | bytes 393220
where the time goes:
time: 80.5 us; the launch traced here: 79.8 us
  blocking collectives  30.2 us (38%)
  starting transfers between devices  16.5 us (20%)
  matrix products  11.5 us (14%)
  other arithmetic  8.01 us (10%)
  local copies, waits for them, and re-layouts  7.03 us (9%)
  between operations  6.46 us (8%)
    all_gather x1, blocking collectives, on_device(): lax.all_gather(joined[0], 'state', axis=0, tiled=True)  12.7 us
    all_gather x1, blocking collectives, on_device(): lax.all_gather(joined[1], 'state', axis=0, tiled=True)  10.1 us
    unnamed x1, blocking collectives  7.37 us
    all_to_all x1, starting transfers between devices, on_device(): lax.all_to_all(place(low_set[2], high_set[2]), 'region', split_axis=0, co...  6.35 us
    dot_general x1, matrix products, add_block(): return jnp.dot(covar, piece_weight, precision=lax.Precision.HIGHEST)  6.17 us
    dot_general x1, matrix products, add_block(): jnp.einsum('rm,pm->rp', flat_state, piece_anom, precision=lax.Precision.H...  5.33 us
    all_to_all x1, starting transfers between devices, on_device(): lax.all_to_all(place(low_set[0], high_set[0]), 'region', split_axis=0, co...  5.11 us
    all_to_all x1, starting transfers between devices, on_device(): lax.all_to_all(place(low_set[1], high_set[1]), 'region', split_axis=0, co...  5.08 us
  transfers between devices with their start and end apart: 3, of which 0 were waited for; matrix products, arithmetic and copies ran while one was open for 19% of the time, Pallas kernels for 0%

commit v1 on v0

--- a/solution.py
+++ b/solution.py
@@ -8,6 +8,28 @@
 HALF = 4
 CAP = 16
 COLS = 256
+
+
+def in_blocks(x, dim, devices):
+    before, after = (x.shape[:dim], x.shape[dim + 1 :])
+    return jnp.moveaxis(x.reshape(*before, devices, -1, *after), dim, 0)
+
+
+def in_order(blocks, dim):
+    blocks = jnp.moveaxis(blocks, 0, dim)
+    shape = blocks.shape
+    return blocks.reshape(*shape[:dim], shape[dim] * shape[dim + 1], *shape[dim + 2 :])
+
+
+def swapped_with_each(value, axis, split_dim, concat_dim):
+    size, here = (lax.axis_size(axis), lax.axis_index(axis))
+    blocks = in_blocks(value, split_dim, size)
+    finished = [blocks[here]]
+    for step in range(1, size):
+        sent = blocks[here ^ step]
+        finished.append(lax.ppermute(sent, axis, [(i, i ^ step) for i in range(size)]))
+    blocks = jnp.stack(finished)[here ^ jnp.arange(size)]
+    return in_order(blocks, concat_dim)
 
 
 def gaspari(scaled):
@@ -75,9 +97,7 @@
         lax.all_to_all(
             place(low_set[1], high_set[1]), "region", split_axis=0, concat_axis=0, tiled=True
         ),
-        lax.all_to_all(
-            place(low_set[2], high_set[2]), "region", split_axis=0, concat_axis=0, tiled=True
-        ),
+        swapped_with_each(place(low_set[2], high_set[2]), "region", 0, 0),
     )
     from_left = tuple(
         (lax.dynamic_index_in_dim(pieces, left_region, 0, keepdims=False) for pieces in slotted)

time: 80.5 us -> 85.9 us (1.067)
  waiting for transfers between devices: 0.01 us -> 4.72 us
  starting transfers between devices: 16.5 us -> 18.2 us
  other arithmetic: 8.01 us -> 6.9 us
    ppermute x0 -> x7, starting transfers between devices: none -> 9.88 us  [swapped_with_each(): lax.ppermute(sent, axis, [(i, i ^ step) for i in range(size)])]
    all_to_all x1 -> x0, starting transfers between devices: 6.35 us -> none  [on_device(): lax.all_to_all(place(low_set[2], high_set[2]), 'region', split_axis=0, co...]
    ppermute x0 -> x7, waiting for transfers between devices: none -> 4.71 us  [swapped_with_each(): lax.ppermute(sent, axis, [(i, i ^ step) for i in range(size)])]
    all_to_all x1, starting transfers between devices: 5.08 us -> 3.41 us  [on_device(): lax.all_to_all(place(low_set[1], high_set[1]), 'region', split_axis=0, co...]
    unnamed x9 -> x20, local copies, waits for them, and re-layouts: 2.8 us -> 2.14 us
    another operation x1 -> x2, local copies, waits for them, and re-layouts: 3.06 us -> 3.09 us
  transfers between devices with their start and end apart: 3 -> 9, of which waited for: 0 -> 2; matrix products, arithmetic and copies ran while one was open for 19% -> 17% of each run, Pallas kernels for 0% -> 0%
where the time goes in v1:
time: 85.9 us; the launch traced here: 85.3 us
  blocking collectives  30 us (35%)
  starting transfers between devices  18.2 us (21%)
  matrix products  11.5 us (13%)
  local copies, waits for them, and re-layouts  6.99 us (8%)
  between operations  6.94 us (8%)
  other arithmetic  6.9 us (8%)
  waiting for transfers between devices  4.72 us (5%)
    all_gather x1, blocking collectives, on_device(): lax.all_gather(joined[0], 'state', axis=0, tiled=True)  12.5 us
    all_gather x1, blocking collectives, on_device(): lax.all_gather(joined[1], 'state', axis=0, tiled=True)  10.1 us
    ppermute x7, starting transfers between devices, swapped_with_each(): lax.ppermute(sent, axis, [(i, i ^ step) for i in range(size)])  9.88 us
    unnamed x1, blocking collectives  7.37 us
    dot_general x1, matrix products, add_block(): return jnp.dot(covar, piece_weight, precision=lax.Precision.HIGHEST)  6.17 us
    dot_general x1, matrix products, add_block(): jnp.einsum('rm,pm->rp', flat_state, piece_anom, precision=lax.Precision.H...  5.32 us
    all_to_all x1, starting transfers between devices, on_device(): lax.all_to_all(place(low_set[0], high_set[0]), 'region', split_axis=0, co...  4.93 us
    ppermute x7, waiting for transfers between devices, swapped_with_each(): lax.ppermute(sent, axis, [(i, i ^ step) for i in range(size)])  4.71 us
  transfers between devices with their start and end apart: 9, of which 2 were waited for; matrix products, arithmetic and copies ran while one was open for 17% of the time, Pallas kernels for 0%

profile of v1, /device:TPU:0, one launch (start us, length us, event | category | flops | bytes accessed | tf_op | source)
XLA Modules:
  0.0 85.3 jit_solution(893192542283246066)
XLA Ops:
  0.0 0.0 copy-start
  0.0 0.0 copy-start.4
  0.0 0.0 copy-start.3
  0.0 1.5 %fusion.10 = s32[]{:T(128)} fusion(s32[8]{0:T(128)} %param.9, s32[]{:T(128)S(6)} %axis_index.19), kind=kLoop, calls=%fused_computation.70 | loop fusion | flops 23 | bytes 40 | tf_op jit(solution)/shard_map/reduce_sum | solution.py:73
  3.5 0.7 broadcast_add_fusion
  4.1 0.1 slice_bitcast_fusion.5
  4.2 1.4 %fusion.11 = (s32[]{:T(128)}, s32[]{:T(128)}) fusion(s32[8]{0:T(128)} %param.9, s32[]{:T(128)S(6)} %select_n.144, s32[]{:T(128)S(6)} %select_n.147), kind=kLoop, calls=%fused_computation.71 | loop fusion | flops 46 | bytes 48 | tf_op jit(solution)/shard_map/reduce_sum | solution.py:74
  5.6 1.3 %iota_compare_fusion = (pred[8]{0:T(512)(128)(4,1)S(1)}, pred[8]{0:T(512)(128)(4,1)S(1)}) fusion(s32[]{:T(128)} %get-tuple-element.6, s32[]{:T(128)} %get-tuple-element.5), kind=kLoop, calls=%fused_computation.81 | loop fusion | flops 16 | bytes 24 | tf_op jit(solution)/shard_map/eq | solution.py:85
  7.0 0.1 select_add_fusion.2
  7.1 0.6 collective-permute-start
  7.6 2.6 %collective-permute-start.1 = (s32[1,16]{1,0:T(1,128)S(1)}, s32[1,16]{1,0:T(1,128)S(1)}, u32[]{:S(2)}, u32[]{:S(2)}) collective-permute-start(s32[1,16]{1,0:T(1,128)S(1)} %get-tuple-element.22), channel_id=1, source_target_pairs={{0,8},{4,12},{8,0},{12,4},{16,24},{20,28},{24,16},{28,20},{1,9},{5... | collective-permute-start | bytes 200 | tf_op jit(solution)/shard_map/ppermute | solution.py:30
  10.3 0.0 collective-permute-start.2
  10.3 2.8 %collective-permute-start.3 = (s32[1,16]{1,0:T(1,128)S(1)}, s32[1,16]{1,0:T(1,128)S(1)}, u32[]{:S(2)}, u32[]{:S(2)}) collective-permute-start(s32[1,16]{1,0:T(1,128)S(1)} %get-tuple-element.20), channel_id=1, source_target_pairs={{0,16},{4,20},{8,24},{12,28},{16,0},{20,4},{24,8},{28,12},{1,17},{... | collective-permute-start | bytes 200 | tf_op jit(solution)/shard_map/ppermute | solution.py:30
  13.1 0.0 collective-permute-start.4
  13.1 0.8 slice_bitcast_fusion.1
  13.9 0.9 %select_add_fusion = (f32[8,16,512]{2,1,0:T(8,128)}, f32[8,16,512]{2,1,0:T(8,128)}) fusion(f32[16,512]{1,0:T(8,128)S(1)} %get-tuple-element.12, f32[16,512]{1,0:T(8,128)S(1)} %get-tuple-element.11, pred[8]{0:T(512)(128)(4,1)S(1)} %get-tuple-element.32, pred[8]{0:T(512)(128)(4,1)S(1)} %get-tuple-element.33, f32[16,512]{1,0:T(8,128)S(1)} %get-tuple-element.34, ...), kind=kLoop, calls=%fused_computation.19 | loop fusion | flops 393216 | bytes 655376 | tf_op jit(solution)/shard_map/add | solution.py:89
  14.8 4.9 %all-to-all-start = ((f32[8,16,512]{2,1,0:T(8,128)}), f32[8,16,512]{2,1,0:T(8,128)S(1)}, u32[]{:S(2)}, u32[]{:S(2)}) async-start(f32[8,16,512]{2,1,0:T(8,128)} %get-tuple-element.27), calls=%async_computation | async-start | bytes 524288 | tf_op jit(solution)/shard_map/all_to_all | solution.py:94
  22.4 0.0 copy-done.3
  23.9 0.0 copy-done.4
  23.9 0.6 dynamic-slice.15
  25.1 0.0 collective-permute-done
  25.1 3.9 %collective-permute-start.5 = (s32[1,16]{1,0:T(1,128)S(1)}, s32[1,16]{1,0:T(1,128)S(1)}, u32[]{:S(2)}, u32[]{:S(2)}) collective-permute-start(s32[1,16]{1,0:T(1,128)S(1)} %get-tuple-element.18), channel_id=1, source_target_pairs={{0,24},{4,28},{8,16},{12,20},{16,8},{20,12},{24,0},{28,4},{1,25},{... | collective-permute-start | bytes 200 | tf_op jit(solution)/shard_map/ppermute | solution.py:30
  29.0 0.0 collective-permute-done.1
  29.0 0.0 collective-permute-start.6
  29.0 0.0 collective-permute-done.2
  29.1 0.0 collective-permute-done.3
  29.1 0.0 collective-permute-done.4
  29.1 1.5 %collective-permute-done.5 = s32[1,16]{1,0:T(1,128)S(1)} collective-permute-done((s32[1,16]{1,0:T(1,128)S(1)}, s32[1,16]{1,0:T(1,128)S(1)}, u32[]{:S(2)}, u32[]{:S(2)}) %collective-permute-start.5) | collective-permute-done | bytes 96 | tf_op jit(solution)/shard_map/ppermute | solution.py:30
  30.6 3.2 %collective-permute-done.6 = s32[1,16]{1,0:T(1,128)S(1)} collective-permute-done((s32[1,16]{1,0:T(1,128)S(1)}, s32[1,16]{1,0:T(1,128)S(1)}, u32[]{:S(2)}, u32[]{:S(2)}) %collective-permute-start.6) | collective-permute-done | bytes 96 | tf_op jit(solution)/shard_map/ppermute | solution.py:30
  33.8 0.6 gather_fusion
  34.4 0.2 add_dynamic-update-slice_fusion
  34.6 7.4 %all-reduce = s32[384]{0:T(512)S(1)} all-reduce(s32[384]{0:T(512)S(1)} %add_dynamic-update-slice_fusion), channel_id=1, replica_groups=mesh['region'=8,'state'=4] {'state'}, use_global_device_ids=true, to_apply=%add | all-reduce | flops 384 | bytes 3072
  42.0 0.8 select_multiply_fusion
  42.8 0.3 mul.120
  43.1 0.0 copy-start.1
  43.1 1.5 %copy.8 = f32[48,8,4,256]{3,1,2,0:T(8,128)} copy(f32[48,8,4,256]{3,2,1,0:T(4,128)S(1)} %bitcast.69) | data formatting | bytes 3145728
  44.5 0.0 all-to-all-done
  44.5 3.4 %all-to-all-start.1 = ((f32[8,16,512]{2,1,0:T(8,128)}), f32[8,16,512]{2,1,0:T(8,128)S(1)}, u32[]{:S(2)}, u32[]{:S(2)}) async-start(f32[8,16,512]{2,1,0:T(8,128)} %get-tuple-element.26), calls=%async_computation.1 | async-start | bytes 524288 | tf_op jit(solution)/shard_map/all_to_all | solution.py:97
  48.0 0.0 copy-done.1
  48.0 12.5 %all_gather.9 = f32[384,512]{1,0:T(8,128)S(1)} all-gather(f32[96,512]{1,0:T(8,128)S(1)} %pad_maximum_fusion), channel_id=1, replica_groups=mesh['region'=8,'state'=4] {'state'}, dimensions={0}, use_global_device_ids=true | all-gather | bytes 983040 | tf_op jit(solution)/shard_map/all_gather | solution.py:126
  60.5 0.0 copy-done
  60.5 5.3 %bitcast_multiply_fusion = f32[1024,384]{0,1:T(8,128)} fusion(f32[1024,384]{0,1:T(8,128)} %bitcast.68, f32[384,512]{1,0:T(8,128)S(1)} %all_gather.9, f32[1024,512]{1,0:T(8,128)S(1)} %bitcast.66), kind=kOutput, calls=%fused_computation.2 | convolution fusion | flops 2416312320 | bytes 6029312 | tf_op jit(solution)/shard_map/rm,pm->rp/dot_general | solution.py:60
  65.8 0.0 copy-start.2
  65.8 3.1 %copy.7 = f32[1024,384]{1,0:T(8,128)} copy(f32[1024,384]{0,1:T(8,128)} %bitcast_multiply_fusion) | data formatting | bytes 3145728 | tf_op jit(solution)/shard_map/reshape.75
  68.9 0.0 all-to-all-done.1
  68.9 0.0 copy-done.2
  69.0 10.1 %all_gather.11 = f32[384,512]{1,0:T(8,128)S(1)} all-gather(f32[96,512]{1,0:T(8,128)S(1)} %pad_maximum_fusion.1), channel_id=1, replica_groups=mesh['region'=8,'state'=4] {'state'}, dimensions={0}, use_global_device_ids=true | all-gather | bytes 983040 | tf_op jit(solution)/shard_map/all_gather | solution.py:127
  79.1 6.2 %convolution_bitcast_fusion = f32[1,4,256,512]{3,2,1,0:T(8,128)} fusion(f32[4,256,384]{2,1,0:T(8,128)} %bitcast.67, f32[384,512]{1,0:T(8,128)S(1)} %all_gather.11), kind=kOutput, calls=%fused_computation.1 | convolution fusion | flops 2415919104 | bytes 4456448 | tf_op jit(solution)/shard_map/dot_general | solution.py:65
  (20 shorter events, 0.2 us)
Async XLA Ops:
  0.0 60.5 %copy-start = (f32[1,4,256,512]{3,2,1,0:T(8,128)S(1)}, f32[1,4,256,512]{3,2,1,0:T(8,128)}, u32[]{:S(2)}) copy-start(f32[1,4,256,512]{3,2,1,0:T(8,128)} %param.5) | copy-start | bytes 6291460
  0.0 23.9 %copy-start.4 = (u32[32]{0:T(128)S(1)}, u32[32]{0:T(128)}, u32[]{:S(2)}) copy-start(u32[32]{0:T(128)} %constant.157) | copy-start | bytes 388
  0.0 22.4 %copy-start.3 = (s32[1,64]{1,0:T(1,128)S(1)}, s32[1,64]{1,0:T(1,128)}, u32[]{:S(2)}) copy-start(s32[1,64]{1,0:T(1,128)} %param.8) | copy-start | bytes 772
  7.1 18.0 %collective-permute-start = (s32[1,16]{1,0:T(1,128)S(1)}, s32[1,16]{1,0:T(1,128)S(1)}, u32[]{:S(2)}, u32[]{:S(2)}) collective-permute-start(s32[1,16]{1,0:T(1,128)S(1)} %get-tuple-element.23), channel_id=1, source_target_pairs={{0,4},{4,0},{8,12},{12,8},{16,20},{20,16},{24,28},{28,24},{1,5},{5... | collective-permute-start | bytes 200 | tf_op jit(solution)/shard_map/ppermute | solution.py:30
  7.6 21.4 %collective-permute-start.1 = (s32[1,16]{1,0:T(1,128)S(1)}, s32[1,16]{1,0:T(1,128)S(1)}, u32[]{:S(2)}, u32[]{:S(2)}) collective-permute-start(s32[1,16]{1,0:T(1,128)S(1)} %get-tuple-element.22), channel_id=1, source_target_pairs={{0,8},{4,12},{8,0},{12,4},{16,24},{20,28},{24,16},{28,20},{1,9},{5... | collective-permute-start | bytes 200 | tf_op jit(solution)/shard_map/ppermute | solution.py:30
  10.3 18.8 %collective-permute-start.2 = (s32[1,16]{1,0:T(1,128)S(1)}, s32[1,16]{1,0:T(1,128)S(1)}, u32[]{:S(2)}, u32[]{:S(2)}) collective-permute-start(s32[1,16]{1,0:T(1,128)S(1)} %get-tuple-element.21), channel_id=1, source_target_pairs={{0,12},{4,8},{8,4},{12,0},{16,28},{20,24},{24,20},{28,16},{1,13},{... | collective-permute-start | bytes 200 | tf_op jit(solution)/shard_map/ppermute | solution.py:30
  10.3 18.7 %collective-permute-start.3 = (s32[1,16]{1,0:T(1,128)S(1)}, s32[1,16]{1,0:T(1,128)S(1)}, u32[]{:S(2)}, u32[]{:S(2)}) collective-permute-start(s32[1,16]{1,0:T(1,128)S(1)} %get-tuple-element.20), channel_id=1, source_target_pairs={{0,16},{4,20},{8,24},{12,28},{16,0},{20,4},{24,8},{28,12},{1,17},{... | collective-permute-start | bytes 200 | tf_op jit(solution)/shard_map/ppermute | solution.py:30
  13.1 16.0 %collective-permute-start.4 = (s32[1,16]{1,0:T(1,128)S(1)}, s32[1,16]{1,0:T(1,128)S(1)}, u32[]{:S(2)}, u32[]{:S(2)}) collective-permute-start(s32[1,16]{1,0:T(1,128)S(1)} %get-tuple-element.19), channel_id=1, source_target_pairs={{0,20},{4,16},{8,28},{12,24},{16,4},{20,0},{24,12},{28,8},{1,21},{... | collective-permute-start | bytes 200 | tf_op jit(solution)/shard_map/ppermute | solution.py:30
  14.8 29.7 %all-to-all-start = ((f32[8,16,512]{2,1,0:T(8,128)}), f32[8,16,512]{2,1,0:T(8,128)S(1)}, u32[]{:S(2)}, u32[]{:S(2)}) async-start(f32[8,16,512]{2,1,0:T(8,128)} %get-tuple-element.27), calls=%async_computation | async-start | bytes 524288 | tf_op jit(solution)/shard_map/all_to_all | solution.py:94
  25.1 5.4 %collective-permute-start.5 = (s32[1,16]{1,0:T(1,128)S(1)}, s32[1,16]{1,0:T(1,128)S(1)}, u32[]{:S(2)}, u32[]{:S(2)}) collective-permute-start(s32[1,16]{1,0:T(1,128)S(1)} %get-tuple-element.18), channel_id=1, source_target_pairs={{0,24},{4,28},{8,16},{12,20},{16,8},{20,12},{24,0},{28,4},{1,25},{... | collective-permute-start | bytes 200 | tf_op jit(solution)/shard_map/ppermute | solution.py:30
  29.0 4.8 %collective-permute-start.6 = (s32[1,16]{1,0:T(1,128)S(1)}, s32[1,16]{1,0:T(1,128)S(1)}, u32[]{:S(2)}, u32[]{:S(2)}) collective-permute-start(s32[1,16]{1,0:T(1,128)S(1)} %get-tuple-element.17), channel_id=1, source_target_pairs={{0,28},{4,24},{8,20},{12,16},{16,12},{20,8},{24,4},{28,0},{1,29},{... | collective-permute-start | bytes 200 | tf_op jit(solution)/shard_map/ppermute | solution.py:30
  43.1 4.9 %copy-start.1 = (f32[1,64,512]{2,1,0:T(8,128)S(1)}, f32[1,64,512]{2,1,0:T(8,128)}, u32[]{:S(2)}) copy-start(f32[1,64,512]{2,1,0:T(8,128)} %param.6) | copy-start | bytes 393220
  44.5 24.4 %all-to-all-start.1 = ((f32[8,16,512]{2,1,0:T(8,128)}), f32[8,16,512]{2,1,0:T(8,128)S(1)}, u32[]{:S(2)}, u32[]{:S(2)}) async-start(f32[8,16,512]{2,1,0:T(8,128)} %get-tuple-element.26), calls=%async_computation.1 | async-start | bytes 524288 | tf_op jit(solution)/shard_map/all_to_all | solution.py:97
  65.8 3.1 %copy-start.2 = (f32[1,64,512]{2,1,0:T(8,128)S(1)}, f32[1,64,512]{2,1,0:T(8,128)}, u32[]{:S(2)}) copy-start(f32[1,64,512]{2,1,0:T(8,128)} %param.7) | copy-start | bytes 393220
